TPU v7x, 512 devices: a whole 4x8x8 slice. The times are simulated.
512 devices in a mesh: doc: 128 (over z_lo, y, x, core), filt: 4 (over z_hi).
Axes of the slice: x: 4, y: 8, z: 8 (z_hi: 4, z_lo: 2; z = z_hi * 2 + z_lo), core: 2. Of those that a mesh axis runs over, the one named last changes fastest.
Arguments:
- embedded: bfloat16 [256, 256, 256], P('doc'), may hold values from -8 to 8
- lengths: int32 [256], P('doc'), may hold values from 1 to 256, 26214 in all
- conv_weight: bfloat16 [256, 15, 1024], P(None, None, 'filt'), may hold values from -0.15625 to 0.15625
- head_weight: bfloat16 [3, 1024], P(None, 'filt'), may hold values from -0.109375 to 0.109375
- occupation: int32 [256], P('doc'), may hold values from 0 to 839
- cohort: int32 [256], P('doc'), may hold values from 0 to 39
- education: int32 [256], P('doc'), may hold values from 0 to 7
- occ_table: float32 [840], replicated, may hold values from -3 to 3
- cohort_table: float32 [40], replicated, may hold values from -3 to 3
- edu_table: float32 [8], replicated, may hold values from -3 to 3
- wage: float32 [256], P('doc'), may hold values from -8 to 8
Outputs:
- conv_grad: float32 [256, 15, 1024], P('doc', None, 'filt')
- head_grad: float32 [3, 1024], P(None, 'filt')
- occ_grad: float32 [840], replicated
- cohort_grad: float32 [40], replicated
- edu_grad: float32 [8], replicated
- prediction: float32 [256], P('doc')
All inputs are finite; a program needn't handle non-finite values. No bound on the sum of `lengths` on one device may be relied on, other than what follows from the above.
Results may differ from a plain program's by a relative error of at most 0.0029.
Values sent between devices are 32-bit elements; how exact they have to be, the bound alone decides.
A program may use at most 64 MiB of HBM per device.

v0:
```python
import jax
import jax.numpy as jnp
from jax import lax
from jax.sharding import PartitionSpec as P

TAU = 0.05
WIDTH_LIST = ((3, 0), (5, 3), (7, 8))


def convolve(columns, weights):
    outputs = []
    for taps, first in WIDTH_LIST:
        half = (taps - 1) // 2
        window = columns[:, :, 3 - half : 3 + half + 1, :]
        outputs.append(
            jnp.einsum(
                "ptje,ejf->ptf",
                window,
                weights[:, first : first + taps, :],
                preferred_element_type=jnp.float32,
            )
        )
    return tuple(outputs)


def grad_terms(columns, slopes):
    outputs = []
    for index in range(3):
        taps = WIDTH_LIST[index][0]
        half = (taps - 1) // 2
        window = columns[:, :, 3 - half : 3 + half + 1, :]
        outputs.append(
            jnp.einsum("ptje,ptf->ejf", window, slopes[index], preferred_element_type=jnp.float32)
        )
    return jnp.concatenate(outputs, axis=1)


def local(
    embedded,
    lengths,
    conv_weight,
    head_weight,
    occupation,
    cohort,
    education,
    occ_table,
    cohort_table,
    edu_table,
    wage,
):
    posts, seq_len, _ = embedded.shape
    positions = jnp.arange(seq_len, dtype=jnp.int32)
    valid = positions[None, :] < lengths[:, None]
    masked = jnp.where(valid[:, :, None], embedded, jnp.zeros_like(embedded))
    padded = jnp.pad(masked, ((0, 0), (3, 3), (0, 0)))
    columns = jnp.stack([padded[:, offset : offset + seq_len, :] for offset in range(7)], axis=2)
    convs = convolve(columns, conv_weight)
    features = []
    shares = []
    for conv in convs:
        score = jnp.where(valid[:, :, None], conv / TAU, -jnp.inf)
        top = jnp.max(score, axis=1, keepdims=True)
        expd = jnp.exp(score - top)
        total = jnp.sum(expd, axis=1, keepdims=True)
        features.append(TAU * (top[:, 0, :] + jnp.log(total[:, 0, :])))
        shares.append(expd / total)
    feature = jnp.stack(features, axis=1)
    head = head_weight.astype(jnp.float32)
    partial_pred = jnp.sum(feature * head[None, :, :], axis=(1, 2))
    occ_hot = (
        occupation[:, None] == jnp.arange(occ_table.shape[0], dtype=jnp.int32)[None, :]
    ).astype(jnp.float32)
    cohort_hot = (
        cohort[:, None] == jnp.arange(cohort_table.shape[0], dtype=jnp.int32)[None, :]
    ).astype(jnp.float32)
    edu_hot = (
        education[:, None] == jnp.arange(edu_table.shape[0], dtype=jnp.int32)[None, :]
    ).astype(jnp.float32)
    highest = lax.Precision.HIGHEST
    offsets = (
        jnp.dot(occ_hot, occ_table, precision=highest)
        + jnp.dot(cohort_hot, cohort_table, precision=highest)
        + jnp.dot(edu_hot, edu_table, precision=highest)
    )
    prediction = lax.psum(partial_pred, "filt") + offsets
    residual = prediction - wage
    slopes = [
        (residual[:, None, None] * head[index][None, None, :] * shares[index]).astype(jnp.bfloat16)
        for index in range(3)
    ]
    conv_grad = lax.psum_scatter(
        grad_terms(columns, slopes), "doc", scatter_dimension=0, tiled=True
    )
    head_terms = jnp.sum(residual[:, None, None] * feature, axis=0)
    head_grad, occ_grad, cohort_grad, edu_grad = lax.psum(
        (
            head_terms,
            jnp.dot(residual, occ_hot, precision=highest),
            jnp.dot(residual, cohort_hot, precision=highest),
            jnp.dot(residual, edu_hot, precision=highest),
        ),
        "doc",
    )
    return (conv_grad, head_grad, occ_grad, cohort_grad, edu_grad, prediction)


def solution(mesh):
    return jax.shard_map(
        local,
        mesh=mesh,
        in_specs=(
            P("doc", None, None),
            P("doc"),
            P(None, None, "filt"),
            P(None, "filt"),
            P("doc"),
            P("doc"),
            P("doc"),
            P(),
            P(),
            P(),
            P("doc"),
        ),
        out_specs=(P("doc", None, "filt"), P(None, "filt"), P(), P(), P(), P("doc")),
        check_vma=False,
    )
```

profile of v0, /device:TPU:1, one launch (start us, length us, event | category | flops | bytes accessed | tf_op | source)
XLA Modules:
  0.0 625.5 jit_solution(2749895344297153735)
XLA Ops:
  7.2 0.8 iota_compare_fusion.3
  8.0 1.1 broadcast_select_fusion
  9.4 0.1 fusion.50
  9.7 0.1 constant_dynamic-update-slice_fusion.1
  10.4 1.6 copy-done.7
  12.0 0.7 fusion.41
  12.7 0.4 copy-done.2
  13.1 0.5 fusion.42
  13.7 0.4 fusion.43
  14.5 16.5 %psum.35 = f32[2]{0:T(128)S(1)} all-reduce(f32[2]{0:T(128)S(1)} %multiply_reduce_fusion.1), channel_id=1, replica_groups=mesh['doc'=128,'filt'=4] {'filt'}, use_global_device_ids=true, to_apply=%region_7.8 | all-reduce | flops 2 | bytes 16 | tf_op jit(solution)/shard_map/psum | solution.py:85
  31.0 0.2 convolution_bitcast_fusion.8
  31.2 0.2 convolution_bitcast_fusion.10
  31.4 0.7 fusion.44
  32.2 2.3 convolution_bitcast_fusion
  34.5 0.6 convolution_bitcast_fusion.1
  35.1 0.4 convolution_bitcast_fusion.2
  35.5 2.1 pad_maximum_fusion
  37.6 5.5 copy.46
  43.2 0.2 convolution_reduce_fusion
  43.4 0.2 convolution_bitcast_fusion.7
  43.6 0.2 convolution_bitcast_fusion.6
  43.8 286.9 %all-reduce.1 = (f32[3,256]{1,0:T(4,128)}, f32[840]{0:T(1024)}, f32[40]{0:T(128)}, f32[8]{0:T(128)}) all-reduce(f32[3,256]{1,0:T(4,128)S(1)} %multiply_reduce_fusion, f32[840]{0:T(1024)S(1)} %convolution_reduce_fusion, f32[40]{0:T(128)S(1)} %convolution_bitcast_fusion.7, ...), channel_id=1, replica_groups=mesh['doc'=128,'filt'=4] {'doc'}, use_global_device_ids=true, to_apply=%region_10.11 | all-reduce | flops 1656 | bytes 13248 | tf_op jit(solution)/shard_map/psum | solution.py:95
  330.7 286.6 %reduce-scatter.2.cloned.1.call-done = f32[2,15,256]{2,1,0:T(8,128)} async-done(((f32[256,15,256]{2,1,0:T(8,128)}), f32[2,15,256]{2,1,0:T(8,128)}) %reduce-scatter.2.cloned.1.call-update) | async-done | bytes 30736 | tf_op jit(solution)/shard_map/reduce_scatter | solution.py:91
  617.3 1.4 copy.47
  (49 shorter events, 1.6 us)
Async XLA Ops:
  7.2 24.2 %copy-start = (f32[40]{0:T(128)S(1)}, f32[40]{0:T(128)}, u32[]{:S(2)}) copy-start(f32[40]{0:T(128)} %param.19) | copy-start | bytes 484
  7.2 2.2 copy-start.1
  7.2 610.1 %reduce-scatter.2.cloned.1.call-start = ((), (), s32[]{:S(2)}) async-start(), calls=%async_computation.1 | async-start | bytes 4227072 | tf_op jit(solution)/shard_map/reduce_scatter | solution.py:91
  9.4 0.7 copy-start.5
  9.8 2.2 copy-start.7
  10.0 2.6 copy-start.4
  12.0 1.1 copy-start.2
  13.6 17.4 %copy-start.6 = (f32[840]{0:T(1024)S(1)}, f32[840]{0:T(1024)}, u32[]{:S(2)}) copy-start(f32[840]{0:T(1024)} %param.18) | copy-start | bytes 10084
  13.6 17.4 %copy-start.8 = (f32[8]{0:T(128)S(1)}, f32[8]{0:T(128)}, u32[]{:S(2)}) copy-start(f32[8]{0:T(128)} %param.20) | copy-start | bytes 100
  13.6 17.4 %copy-start.12 = (s32[2]{0:T(128)S(1)}, s32[2]{0:T(128)}, u32[]{:S(2)}) copy-start(s32[2]{0:T(128)} %param.17) | copy-start | bytes 28
  13.6 17.6 %copy-start.10 = (s32[2]{0:T(128)S(1)}, s32[2]{0:T(128)}, u32[]{:S(2)}) copy-start(s32[2]{0:T(128)} %param.15) | copy-start | bytes 28
  13.6 17.8 %copy-start.9 = (f32[2]{0:T(128)S(1)}, f32[2]{0:T(128)}, u32[]{:S(2)}) copy-start(f32[2]{0:T(128)} %param.21) | copy-start | bytes 28
  13.7 17.8 %copy-start.11 = (s32[2]{0:T(128)S(1)}, s32[2]{0:T(128)}, u32[]{:S(2)}) copy-start(s32[2]{0:T(128)} %param.16) | copy-start | bytes 28
  32.2 2.3 copy-start.3
Sparse Core Ops, SparseCore 0:
  43.3 573.9 reduce-scatter.1
where the time goes:
time: 628 us; the launch traced here: 626 us
  blocking collectives  303 us (48%)
  waiting for transfers between devices  287 us (46%)
  between operations  14.3 us (2%)
  local copies, waits for them, and re-layouts  9.74 us (2%)
  matrix products  6.49 us (1%)
    psum x1, blocking collectives, local(): lax.psum((head_terms, jnp.dot(residual, occ_hot, precision=highest), jnp....  287 us
    reduce_scatter x1, waiting for transfers between devices, local(): lax.psum_scatter(grad_terms(columns, slopes), 'doc', scatter_dimension=0,...  287 us
    psum x1, blocking collectives, local(): prediction = lax.psum(partial_pred, 'filt') + offsets  16.5 us
  transfers between devices with their start and end apart: 1, of which 1 were waited for; matrix products, arithmetic and copies ran while one was open for 0% of the time, Pallas kernels for 0%

commit v1 on v0

--- a/solution.py
+++ b/solution.py
@@ -1,10 +1,16 @@
 import jax
 import jax.numpy as jnp
 from jax import lax
+from jax.experimental import pallas as pl
+from jax.experimental.pallas import tpu as pltpu
 from jax.sharding import PartitionSpec as P
 
 TAU = 0.05
 WIDTH_LIST = ((3, 0), (5, 3), (7, 8))
+NZ, NY, NX = 2, 8, 4
+HALF_ROWS = 4096
+KEEP = 2048
+F32 = jnp.float32
 
 
 def convolve(columns, weights):
@@ -23,16 +29,236 @@
     return tuple(outputs)
 
 
-def grad_terms(columns, slopes):
-    outputs = []
-    for index in range(3):
-        taps = WIDTH_LIST[index][0]
-        half = (taps - 1) // 2
-        window = columns[:, :, 3 - half : 3 + half + 1, :]
-        outputs.append(
-            jnp.einsum("ptje,ptf->ejf", window, slopes[index], preferred_element_type=jnp.float32)
-        )
-    return jnp.concatenate(outputs, axis=1)
+def kernel(
+    occ_ref, coh_ref, edu_ref, rows_ref, feat_ref, head_ref, cols_ref, share_ref,
+    conv_out, small_out, pred_out,
+    pred_buf, slope, grad, from_core, kept, from_y, from_xa, from_xb, from_yb, from_z,
+    sums, sum_core, sum_z, sum_x, sum_y,
+    pred_send, pred_recv, core_send, core_recv, chain_send, chain_recv,
+    xa_send, xa_recv, xb_send, xb_recv, yb_send, yb_recv, z_send, z_recv,
+    s_send, s_recv, sx_send, sx_recv, sy_send, sy_recv,
+):
+    doc = lax.axis_index("doc")
+    filt = lax.axis_index("filt")
+    c = lax.rem(doc, 2)
+    x = lax.rem(doc // 2, NX)
+    y = lax.rem(doc // (2 * NX), NY)
+    z = doc // (2 * NX * NY)
+
+    def at(z_to, y_to, x_to, c_to):
+        return {"doc": ((z_to * NY + y_to) * NX + x_to) * 2 + c_to}
+
+    def x_plus(d):
+        return lax.rem(x + d, NX)
+
+    def y_plus(d):
+        return lax.rem(y + d, NY)
+
+    core_to = at(z, y, x, 1 - c)
+    z_to = at(1 - z, y, x, c)
+    x_to = [at(z, y, x_plus(d), c) for d in range(1, NX)]
+    y_to = [at(z, y_plus(d), x, c) for d in range(1, NY)]
+    filt_to = [{"filt": lax.rem(filt + d, 4)} for d in range(1, 4)]
+
+    barrier = pltpu.get_barrier_semaphore()
+    partners = [core_to, z_to] + x_to + y_to + filt_to
+    for to in partners:
+        pl.semaphore_signal(barrier, inc=1, device_id=to, device_id_type=pl.DeviceIdType.MESH)
+    pl.semaphore_wait(barrier, len(partners))
+
+    started = []
+
+    def send(src, dst, send_sem, recv_sem, to):
+        copy = pltpu.make_async_remote_copy(
+            src_ref=src, dst_ref=dst, send_sem=send_sem, recv_sem=recv_sem,
+            device_id=to, device_id_type=pl.DeviceIdType.MESH,
+        )
+        copy.start()
+        started.append(copy)
+        return copy
+
+    pred_copies = [
+        send(rows_ref.at[0], pred_buf.at[filt], pred_send.at[d], pred_recv.at[d], filt_to[d])
+        for d in range(3)
+    ]
+    pred_buf[filt] = rows_ref[0]
+    for copy in pred_copies:
+        copy.wait_recv()
+    pred = pred_buf[0] + pred_buf[1] + pred_buf[2] + pred_buf[3] + rows_ref[1]
+    pred_out[...] = pred
+    resid = pred - rows_ref[2]
+
+    grid_row = lax.broadcasted_iota(jnp.int32, (8, 256), 0)
+    grid_lane = lax.broadcasted_iota(jnp.int32, (8, 256), 1)
+    small = jnp.zeros((8, 256), F32)
+    for p in range(2):
+        r = resid[p : p + 1, :]
+        r = jnp.concatenate([r, r], axis=1)
+        for w in range(3):
+            scale = r * head_ref[w : w + 1, :].astype(F32)
+            value = (scale * share_ref[w, p]).astype(jnp.bfloat16)
+            for h in range(2):
+                slope[h, p * 256 : (p + 1) * 256, w * 128 : (w + 1) * 128] = value[
+                    :, h * 128 : (h + 1) * 128
+                ]
+        rb = jnp.broadcast_to(r, (8, 256))
+        zero = jnp.zeros((8, 256), F32)
+        small += rb * feat_ref[p]
+        small += jnp.where((grid_row - 4) * 256 + grid_lane == occ_ref[p], rb, zero)
+        small += jnp.where((grid_row == 3) & (grid_lane == coh_ref[p]), rb, zero)
+        small += jnp.where((grid_row == 3) & (grid_lane - 128 == edu_ref[p]), rb, zero)
+    sums[0] = small
+    s_core = send(sums.at[0], sum_core, s_send.at[0], s_recv.at[0], core_to)
+
+    core_copies = []
+    for h in range(2):
+        base = h * HALF_ROWS
+        for k in range(7):
+            low = max(0, abs(k - 3) - 1)
+            part = lax.dot_general(
+                cols_ref[k, :, h * 256 : (h + 1) * 256],
+                slope[h, :, low * 128 :],
+                (((0,), (0,)), ((), ())),
+                preferred_element_type=F32,
+            )
+            for w in range(low, 3):
+                taps, first = WIDTH_LIST[w]
+                tap = first + k - 3 + (taps - 1) // 2
+                grad[pl.ds(base + tap, 256, stride=16), :] = part[
+                    :, (w - low) * 128 : (w - low + 1) * 128
+                ]
+        grad[pl.ds(base + 15, 256, stride=16), :] = jnp.zeros((256, 128), F32)
+        core_copies.append(
+            send(
+                grad.at[pl.ds(base + (1 - c) * KEEP, KEEP)],
+                from_core.at[h], core_send.at[h], core_recv.at[h], core_to,
+            )
+        )
+
+    def take_core(h):
+        core_copies[h].wait_recv()
+
+        @pl.loop(0, KEEP // 256)
+        def _(b):
+            rows = pl.ds(b * 256, 256)
+            mine = pl.ds(h * HALF_ROWS + c * KEEP + b * 256, 256)
+            kept[h, rows, :] = grad[mine, :] + from_core[h, rows, :]
+
+    counts = ((4, 3), (3, 4))
+    chain = {}
+
+    def chain_rows(u, owner):
+        return pl.ds(owner * 256 + u * 128, 128)
+
+    def chain_step(s):
+        for u in range(2):
+            for way in range(2):
+                n = counts[u][way]
+                if s >= n:
+                    continue
+                owner = y_plus(n - s) if way == 0 else y_plus(NY - n + s)
+                rows = chain_rows(u, owner)
+                if s > 0:
+                    chain[u, way, s - 1].wait_recv()
+                    kept[0, rows, :] = kept[0, rows, :] + from_y[u, way, s - 1]
+                chain[u, way, s] = send(
+                    kept.at[0, rows], from_y.at[u, way, s],
+                    chain_send.at[u, way, s], chain_recv.at[u, way, s],
+                    y_to[0] if way == 0 else y_to[NY - 2],
+                )
+
+    take_core(0)
+    chain_step(0)
+    take_core(1)
+    xb = [
+        send(
+            kept.at[1, pl.ds(x_plus(d) * 512, 512)], from_xb.at[d - 1],
+            xb_send.at[d - 1], xb_recv.at[d - 1], x_to[d - 1],
+        )
+        for d in range(1, NX)
+    ]
+    s_core.wait_recv()
+    sums[1] = sums[0] + sum_core[...]
+    s_z = send(sums.at[1], sum_z, s_send.at[1], s_recv.at[1], z_to)
+    chain_step(1)
+    s_z.wait_recv()
+    sums[2] = sums[1] + sum_z[...]
+    sum_x[x] = sums[2]
+    sx = [
+        send(sums.at[2], sum_x.at[x], sx_send.at[d - 1], sx_recv.at[d - 1], x_to[d - 1])
+        for d in range(1, NX)
+    ]
+    chain_step(2)
+    for copy in sx:
+        copy.wait_recv()
+    sums[3] = sum_x[0] + sum_x[1] + sum_x[2] + sum_x[3]
+    sum_y[y] = sums[3]
+    sy = [
+        send(sums.at[3], sum_y.at[y], sy_send.at[d - 1], sy_recv.at[d - 1], y_to[d - 1])
+        for d in range(1, NY)
+    ]
+    chain_step(3)
+
+    for copy in xb:
+        copy.wait_recv()
+    mine_x = pl.ds(x * 512, 512)
+    kept[1, mine_x, :] = kept[1, mine_x, :] + from_xb[0] + from_xb[1] + from_xb[2]
+    yb = [
+        send(
+            kept.at[1, pl.ds(x * 512 + y_plus(d) * 64, 64)], from_yb.at[d - 1],
+            yb_send.at[d - 1], yb_recv.at[d - 1], y_to[d - 1],
+        )
+        for d in range(1, NY)
+    ]
+
+    for u in range(2):
+        rows = chain_rows(u, y)
+        total = kept[0, rows, :]
+        for way in range(2):
+            last = counts[u][way] - 1
+            chain[u, way, last].wait_recv()
+            total += from_y[u, way, last]
+        kept[0, rows, :] = total
+    xa = [
+        send(
+            kept.at[0, pl.ds(y * 256 + x_plus(d) * 64, 64)], from_xa.at[d - 1],
+            xa_send.at[d - 1], xa_recv.at[d - 1], x_to[d - 1],
+        )
+        for d in range(1, NX)
+    ]
+
+    for copy in xa:
+        copy.wait_recv()
+    row_a = y * 256 + x * 64
+    rows = pl.ds(row_a, 64)
+    kept[0, rows, :] = kept[0, rows, :] + from_xa[0] + from_xa[1] + from_xa[2]
+    za = send(kept.at[0, pl.ds(row_a + (1 - z) * 32, 32)], from_z.at[0], z_send.at[0], z_recv.at[0], z_to)
+    for copy in yb:
+        copy.wait_recv()
+    row_b = x * 512 + y * 64
+    rows = pl.ds(row_b, 64)
+    total = kept[1, rows, :]
+    for d in range(NY - 1):
+        total += from_yb[d]
+    kept[1, rows, :] = total
+    zb = send(kept.at[1, pl.ds(row_b + (1 - z) * 32, 32)], from_z.at[1], z_send.at[1], z_recv.at[1], z_to)
+    for copy in sy:
+        copy.wait_recv()
+    total = sum_y[0]
+    for d in range(1, NY):
+        total += sum_y[d]
+    small_out[...] = total
+    for h, (copy, row) in enumerate(((za, row_a), (zb, row_b))):
+        copy.wait_recv()
+        value = kept[h, pl.ds(row + z * 32, 32), :] + from_z[h]
+        for i in range(2):
+            conv_out[i, :, h * 128 : (h + 1) * 128] = value[i * 16 : (i + 1) * 16, :]
+    for copy in started:
+        copy.wait_send()
+
+
+def rows8(values):
+    return jnp.pad(jnp.broadcast_to(values[:, None], (2, 128)), ((0, 6), (0, 0)))
 
 
 def local(
@@ -76,32 +302,77 @@
     edu_hot = (
         education[:, None] == jnp.arange(edu_table.shape[0], dtype=jnp.int32)[None, :]
     ).astype(jnp.float32)
-    highest = lax.Precision.HIGHEST
     offsets = (
-        jnp.dot(occ_hot, occ_table, precision=highest)
-        + jnp.dot(cohort_hot, cohort_table, precision=highest)
-        + jnp.dot(edu_hot, edu_table, precision=highest)
+        jnp.sum(occ_hot * occ_table[None, :], axis=1)
+        + jnp.sum(cohort_hot * cohort_table[None, :], axis=1)
+        + jnp.sum(edu_hot * edu_table[None, :], axis=1)
     )
-    prediction = lax.psum(partial_pred, "filt") + offsets
-    residual = prediction - wage
-    slopes = [
-        (residual[:, None, None] * head[index][None, None, :] * shares[index]).astype(jnp.bfloat16)
-        for index in range(3)
-    ]
-    conv_grad = lax.psum_scatter(
-        grad_terms(columns, slopes), "doc", scatter_dimension=0, tiled=True
+
+    e = jnp.arange(256, dtype=jnp.int32)[:, None]
+    spot = jnp.arange(512, dtype=jnp.int32)[None, :]
+    i, c, x, y, z = e % 2, (e // 2) % 2, (e // 4) % 4, (e // 16) % 8, e // 128
+    place_a = c * 128 + y * 16 + x * 4 + z * 2 + i
+    place_b = 256 + c * 128 + x * 32 + y * 4 + z * 2 + i
+    picks = ((spot == place_a) | (spot == place_b)).astype(jnp.bfloat16)
+    ordered = jnp.einsum(
+        "pte,ek->ptk", masked, picks, preferred_element_type=jnp.float32
+    ).astype(jnp.bfloat16)
+    ordered = jnp.pad(ordered, ((0, 0), (3, 3), (0, 0)))
+    cols = jnp.stack(
+        [ordered[:, offset : offset + seq_len, :] for offset in range(7)], axis=0
+    ).reshape(7, posts * seq_len, 512)
+
+    vmem = pl.BlockSpec(memory_space=pltpu.VMEM)
+    smem = pl.BlockSpec(memory_space=pltpu.SMEM)
+    dma = pltpu.SemaphoreType.DMA
+    conv_grad, small, pred = pl.pallas_call(
+        kernel,
+        out_shape=(
+            jax.ShapeDtypeStruct((2, 16, 256), F32),
+            jax.ShapeDtypeStruct((8, 256), F32),
+            jax.ShapeDtypeStruct((8, 128), F32),
+        ),
+        in_specs=[smem] * 3 + [vmem] * 5,
+        out_specs=(vmem, vmem, vmem),
+        scratch_shapes=[
+            pltpu.VMEM((4, 8, 128), F32),
+            pltpu.VMEM((2, 512, 384), jnp.bfloat16),
+            pltpu.VMEM((2 * HALF_ROWS, 128), F32),
+            pltpu.VMEM((2, KEEP, 128), F32),
+            pltpu.VMEM((2, KEEP, 128), F32),
+            pltpu.VMEM((2, 2, 4, 128, 128), F32),
+            pltpu.VMEM((3, 64, 128), F32),
+            pltpu.VMEM((3, 512, 128), F32),
+            pltpu.VMEM((7, 64, 128), F32),
+            pltpu.VMEM((2, 32, 128), F32),
+            pltpu.VMEM((4, 8, 256), F32),
+            pltpu.VMEM((8, 256), F32),
+            pltpu.VMEM((8, 256), F32),
+            pltpu.VMEM((NX, 8, 256), F32),
+            pltpu.VMEM((NY, 8, 256), F32),
+            dma((3,)), dma((3,)), dma((2,)), dma((2,)), dma((2, 2, 4)), dma((2, 2, 4)),
+            dma((3,)), dma((3,)), dma((3,)), dma((3,)), dma((7,)), dma((7,)), dma((2,)), dma((2,)),
+            dma((2,)), dma((2,)), dma((3,)), dma((3,)), dma((7,)), dma((7,)),
+        ],
+        compiler_params=pltpu.CompilerParams(
+            collective_id=0, has_side_effects=True, vmem_limit_bytes=40 * 1024 * 1024
+        ),
+    )(
+        occupation, cohort, education,
+        jnp.stack([rows8(partial_pred), rows8(offsets), rows8(wage)]),
+        jnp.pad(feature, ((0, 0), (0, 5), (0, 0))),
+        head_weight,
+        cols,
+        jnp.stack(shares),
     )
-    head_terms = jnp.sum(residual[:, None, None] * feature, axis=0)
-    head_grad, occ_grad, cohort_grad, edu_grad = lax.psum(
-        (
-            head_terms,
-            jnp.dot(residual, occ_hot, precision=highest),
-            jnp.dot(residual, cohort_hot, precision=highest),
-            jnp.dot(residual, edu_hot, precision=highest),
-        ),
-        "doc",
+    return (
+        conv_grad[:, :15, :],
+        small[:3],
+        small[4:].reshape(1024)[:840],
+        small[3, :40],
+        small[3, 128:136],
+        pred[:2, 0],
     )
-    return (conv_grad, head_grad, occ_grad, cohort_grad, edu_grad, prediction)
 
 
 def solution(mesh):

time: 628 us -> 67.5 us (0.11)
  blocking collectives: 303 us -> 0 us
  waiting for transfers between devices: 287 us -> 0 us
  Pallas kernels: 0 us -> 54 us
  between operations: 14.3 us -> 1 us
    psum x2 -> x0, blocking collectives: 303 us -> none  [the longest x1 287 us: local(): lax.psum((head_terms, jnp.dot(residual, occ_hot, precision=highest), jnp....]
    reduce_scatter x1 -> x0, waiting for transfers between devices: 287 us -> none  [local(): lax.psum_scatter(grad_terms(columns, slopes), 'doc', scatter_dimension=0,...]
    pallas_call x0 -> x1, Pallas kernels: none -> 54 us  [local(): pl.pallas_call(kernel, out_shape=(jax.ShapeDtypeStruct((2, 16, 256), F32)...]
  transfers between devices with their start and end apart: 1 -> 0, of which waited for: 1 -> 0; matrix products, arithmetic and copies ran while one was open for 0% -> 0% of each run, Pallas kernels for 0% -> 0%
where the time goes in v1:
time: 67.5 us; the launch traced here: 67.3 us
  Pallas kernels  54 us (80%)
  local copies, waits for them, and re-layouts  6.8 us (10%)
  other arithmetic  3.49 us (5%)
  matrix products  2.04 us (3%)
  between operations  1 us (1%)
    pallas_call x1, Pallas kernels, local(): pl.pallas_call(kernel, out_shape=(jax.ShapeDtypeStruct((2, 16, 256), F32)...  54 us
    unnamed x35, local copies, waits for them, and re-layouts  3.32 us
    dot_general x3, matrix products, convolve(): jnp.einsum('ptje,ejf->ptf', window, weights[:, first:first + taps, :], pr...  1.57 us

profile of v1, /device:TPU:1, one launch (start us, length us, event | category | flops | bytes accessed | tf_op | source)
XLA Modules:
  0.0 67.3 jit_solution(18262314350843621648)
XLA Ops:
  0.6 0.7 %iota_compare_fusion.3 = pred[2,256]{1,0:T(4,128)(4,1)S(1)} fusion(s32[2]{0:T(128)} %param.12), kind=kLoop, calls=%fused_computation.89 | loop fusion | flops 512 | bytes 520 | tf_op jit(solution)/shard_map/lt | solution.py:279
  1.4 1.2 %broadcast_select_fusion = bf16[2,256,256]{2,1,0:T(8,128)(2,1)S(1)} fusion(bf16[2,256,256]{2,1,0:T(8,128)(2,1)} %param.11, pred[2,256]{1,0:T(4,128)(4,1)S(1)} %iota_compare_fusion.3), kind=kLoop, calls=%fused_computation.52 | loop fusion | flops 131072 | bytes 524800 | tf_op jit(solution)/shard_map/jit(_where)/select_n | solution.py:280
  3.0 0.1 constant_dynamic-update-slice_fusion.4
  3.1 0.1 bitcast_dynamic-update-slice_fusion.10
  3.2 1.0 %copy-done.6 = bf16[256,15,256]{2,0,1:T(8,128)(2,1)S(1)} copy-done((bf16[256,15,256]{2,0,1:T(8,128)(2,1)S(1)}, bf16[256,15,256]{2,0,1:T(8,128)(2,1)}, u32[]{:S(2)}) %copy-start.6) | copy-done | bytes 1966104
  4.2 0.5 fusion.38
  5.0 0.7 fusion.37
  5.7 0.2 divide_bitcast_fusion
  6.0 0.1 fusion.43
  6.1 0.4 fusion.39
  6.9 0.5 convolution_convert_fusion
  7.3 0.7 %pad_slice_fusion = (bf16[2,256,512]{2,1,0:T(8,128)(2,1)S(1)}, bf16[2,256,512]{2,1,0:T(8,128)(2,1)S(1)}, bf16[2,256,512]{2,1,0:T(8,128)(2,1)S(1)}, bf16[2,256,51...) fusion(bf16[2,256,512]{2,1,0:T(8,128)(2,1)S(1)} %convolution_convert_fusion), kind=kLoop, calls=%fused_computation.53 | loop fusion | bytes 3670016 | tf_op jit(solution)/shard_map/slice | solution.py:322
  8.5 0.4 copy-done
  8.9 0.1 pad_maximum_fusion.2
  9.1 0.2 fusion.25
  9.3 0.2 fusion.28
  9.5 0.2 fusion.29
  9.8 54.0 %shard_map.154 = (f32[2,16,256]{2,1,0:T(8,128)S(1)}, f32[8,256]{1,0:T(8,128)S(1)}, f32[8,128]{1,0:T(8,128)S(1)}) custom-call(s32[2]{0:T(128)S(1)} %copy-done.1, s32[2]{0:T(128)S(1)} %copy-done.2, s32[2]{0:T(128)S(1)} %copy-done.3, f32[3,8,128]{2,1,0:T(8,128)S(1)} %pad_maximum_fusion.1.rows_ref, f32[2,8,256]{2,1,0:T(8,128)S(1)} %pad.26.feat_ref, ...), custom_call_target="tpu_custom_call" | custom-call | tf_op jit(solution)/shard_map/pallas_call | solution.py:328
  63.8 0.6 copy.31
  64.5 0.6 copy.35
  65.1 0.6 slice.88
  65.7 0.5 slice_bitcast_fusion.3
  66.2 0.5 slice_bitcast_fusion.4
  66.7 0.6 slice_reduce_fusion
  (56 shorter events, 1.7 us)
Async XLA Ops:
  1.4 1.6 %copy-start.4 = (bf16[2,256,256]{2,1,0:T(8,128)(2,1)S(1)}, bf16[2,256,256]{2,1,0:T(8,128)(2,1)}, u32[]{:S(2)}) copy-start(bf16[2,256,256]{2,1,0:T(8,128)(2,1)} %param.11) | copy-start | bytes 786436
  2.7 1.5 %copy-start.6 = (bf16[256,15,256]{2,0,1:T(8,128)(2,1)S(1)}, bf16[256,15,256]{2,0,1:T(8,128)(2,1)}, u32[]{:S(2)}) copy-start(bf16[256,15,256]{2,0,1:T(8,128)(2,1)} %param.13) | copy-start | bytes 5898244
  8.2 0.7 %copy-start = (bf16[3,256]{1,0:T(4,128)(2,1)S(1)}, bf16[3,256]{1,0:T(4,128)(2,1)}, u32[]{:S(2)}) copy-start(bf16[3,256]{1,0:T(4,128)(2,1)} %head_ref.1) | copy-start | bytes 4612
  8.2 0.9 %copy-start.1 = (s32[2]{0:T(128)S(1)}, s32[2]{0:T(128)}, u32[]{:S(2)}) copy-start(s32[2]{0:T(128)} %occ_ref.1) | copy-start | bytes 28
  8.2 0.9 %copy-start.5 = (f32[840]{0:T(1024)S(1)}, f32[840]{0:T(1024)}, u32[]{:S(2)}) copy-start(f32[840]{0:T(1024)} %param.18) | copy-start | bytes 10084
  8.2 1.0 %copy-start.2 = (s32[2]{0:T(128)S(1)}, s32[2]{0:T(128)}, u32[]{:S(2)}) copy-start(s32[2]{0:T(128)} %coh_ref.1) | copy-start | bytes 28
  8.2 1.0 %copy-start.7 = (f32[40]{0:T(128)S(1)}, f32[40]{0:T(128)}, u32[]{:S(2)}) copy-start(f32[40]{0:T(128)} %param.19) | copy-start | bytes 484
  8.3 1.2 %copy-start.3 = (s32[2]{0:T(128)S(1)}, s32[2]{0:T(128)}, u32[]{:S(2)}) copy-start(s32[2]{0:T(128)} %edu_ref.1) | copy-start | bytes 28
  8.3 1.2 %copy-start.8 = (f32[8]{0:T(128)S(1)}, f32[8]{0:T(128)}, u32[]{:S(2)}) copy-start(f32[8]{0:T(128)} %param.20) | copy-start | bytes 100
  8.3 1.5 %copy-start.9 = (f32[2]{0:T(128)S(1)}, f32[2]{0:T(128)}, u32[]{:S(2)}) copy-start(f32[2]{0:T(128)} %param.21) | copy-start | bytes 28

commit v2 on v1

--- a/solution.py
+++ b/solution.py
@@ -32,7 +32,7 @@
 def kernel(
     occ_ref, coh_ref, edu_ref, rows_ref, feat_ref, head_ref, cols_ref, share_ref,
     conv_out, small_out, pred_out,
-    pred_buf, slope, grad, from_core, kept, from_y, from_xa, from_xb, from_yb, from_z,
+    pred_buf, slope, grad, from_core, kept, from_y, from_xa, from_xb, from_yb, from_za, from_zb,
     sums, sum_core, sum_z, sum_x, sum_y,
     pred_send, pred_recv, core_send, core_recv, chain_send, chain_recv,
     xa_send, xa_recv, xb_send, xb_recv, yb_send, yb_recv, z_send, z_recv,
@@ -167,20 +167,38 @@
                     y_to[0] if way == 0 else y_to[NY - 2],
                 )
 
+    b_counts = ((2, 1), (1, 2))
+    b_chain = {}
+
+    def b_rows(u, owner):
+        return pl.ds(owner * 512 + u * 256, 256)
+
+    def b_step(s):
+        for u in range(2):
+            for way in range(2):
+                n = b_counts[u][way]
+                if s >= n:
+                    continue
+                owner = x_plus(n - s) if way == 0 else x_plus(NX - n + s)
+                rows = b_rows(u, owner)
+                if s > 0:
+                    b_chain[u, way, s - 1].wait_recv()
+                    kept[1, rows, :] = kept[1, rows, :] + from_xb[u, way, s - 1]
+                b_chain[u, way, s] = send(
+                    kept.at[1, rows], from_xb.at[u, way, s],
+                    xb_send.at[u, way, s], xb_recv.at[u, way, s],
+                    x_to[0] if way == 0 else x_to[NX - 2],
+                )
+
     take_core(0)
     chain_step(0)
     take_core(1)
-    xb = [
-        send(
-            kept.at[1, pl.ds(x_plus(d) * 512, 512)], from_xb.at[d - 1],
-            xb_send.at[d - 1], xb_recv.at[d - 1], x_to[d - 1],
-        )
-        for d in range(1, NX)
-    ]
+    b_step(0)
     s_core.wait_recv()
     sums[1] = sums[0] + sum_core[...]
     s_z = send(sums.at[1], sum_z, s_send.at[1], s_recv.at[1], z_to)
     chain_step(1)
+    b_step(1)
     s_z.wait_recv()
     sums[2] = sums[1] + sum_z[...]
     sum_x[x] = sums[2]
@@ -199,17 +217,17 @@
     ]
     chain_step(3)
 
-    for copy in xb:
-        copy.wait_recv()
-    mine_x = pl.ds(x * 512, 512)
-    kept[1, mine_x, :] = kept[1, mine_x, :] + from_xb[0] + from_xb[1] + from_xb[2]
-    yb = [
-        send(
-            kept.at[1, pl.ds(x * 512 + y_plus(d) * 64, 64)], from_yb.at[d - 1],
-            yb_send.at[d - 1], yb_recv.at[d - 1], y_to[d - 1],
-        )
-        for d in range(1, NY)
-    ]
+    for u in range(2):
+        rows = b_rows(u, x)
+        total = kept[1, rows, :]
+        for way in range(2):
+            last = b_counts[u][way] - 1
+            b_chain[u, way, last].wait_recv()
+            total += from_xb[u, way, last]
+        kept[1, rows, :] = total
+    zb = send(
+        kept.at[1, pl.ds(x * 512 + (1 - z) * 256, 256)], from_zb, z_send.at[1], z_recv.at[1], z_to
+    )
 
     for u in range(2):
         rows = chain_rows(u, y)
@@ -227,34 +245,54 @@
         for d in range(1, NX)
     ]
 
+    zb.wait_recv()
+    row_b = x * 512 + z * 256
+    rows = pl.ds(row_b, 256)
+    kept[1, rows, :] = kept[1, rows, :] + from_zb[...]
+    yb = [
+        send(
+            kept.at[1, pl.ds(row_b + y_plus(d) * 32, 32)], from_yb.at[d - 1],
+            yb_send.at[d - 1], yb_recv.at[d - 1], y_to[d - 1],
+        )
+        for d in range(1, NY)
+    ]
+
     for copy in xa:
         copy.wait_recv()
     row_a = y * 256 + x * 64
     rows = pl.ds(row_a, 64)
     kept[0, rows, :] = kept[0, rows, :] + from_xa[0] + from_xa[1] + from_xa[2]
-    za = send(kept.at[0, pl.ds(row_a + (1 - z) * 32, 32)], from_z.at[0], z_send.at[0], z_recv.at[0], z_to)
-    for copy in yb:
-        copy.wait_recv()
-    row_b = x * 512 + y * 64
-    rows = pl.ds(row_b, 64)
-    total = kept[1, rows, :]
-    for d in range(NY - 1):
-        total += from_yb[d]
-    kept[1, rows, :] = total
-    zb = send(kept.at[1, pl.ds(row_b + (1 - z) * 32, 32)], from_z.at[1], z_send.at[1], z_recv.at[1], z_to)
+    za = send(kept.at[0, pl.ds(row_a + (1 - z) * 32, 32)], from_za, z_send.at[0], z_recv.at[0], z_to)
     for copy in sy:
         copy.wait_recv()
     total = sum_y[0]
     for d in range(1, NY):
         total += sum_y[d]
     small_out[...] = total
-    for h, (copy, row) in enumerate(((za, row_a), (zb, row_b))):
+    for copy in yb:
         copy.wait_recv()
-        value = kept[h, pl.ds(row + z * 32, 32), :] + from_z[h]
+    second = kept[1, pl.ds(row_b + y * 32, 32), :]
+    for d in range(NY - 1):
+        second += from_yb[d]
+    za.wait_recv()
+    first = kept[0, pl.ds(row_a + z * 32, 32), :] + from_za[...]
+    for h, value in enumerate((first, second)):
         for i in range(2):
             conv_out[i, :, h * 128 : (h + 1) * 128] = value[i * 16 : (i + 1) * 16, :]
     for copy in started:
         copy.wait_send()
+
+
+def place_kernel(conv_ref, small_ref, pred_ref, conv_out, head_out, occ_out, coh_out, edu_out, pred_out):
+    for i in range(2):
+        conv_out[:, i, :] = conv_ref[i, :15, :]
+        pred_out[i] = pred_ref[i, 0]
+    head_out[...] = small_ref[:3, :]
+    for k in range(4):
+        size = min(256, 840 - 256 * k)
+        occ_out[256 * k : 256 * k + size] = small_ref[4 + k, :size]
+    coh_out[...] = small_ref[3, :40]
+    edu_out[...] = small_ref[3, 128:136]
 
 
 def rows8(values):
@@ -312,7 +350,7 @@
     spot = jnp.arange(512, dtype=jnp.int32)[None, :]
     i, c, x, y, z = e % 2, (e // 2) % 2, (e // 4) % 4, (e // 16) % 8, e // 128
     place_a = c * 128 + y * 16 + x * 4 + z * 2 + i
-    place_b = 256 + c * 128 + x * 32 + y * 4 + z * 2 + i
+    place_b = 256 + c * 128 + x * 32 + z * 16 + y * 2 + i
     picks = ((spot == place_a) | (spot == place_b)).astype(jnp.bfloat16)
     ordered = jnp.einsum(
         "pte,ek->ptk", masked, picks, preferred_element_type=jnp.float32
@@ -342,16 +380,17 @@
             pltpu.VMEM((2, KEEP, 128), F32),
             pltpu.VMEM((2, 2, 4, 128, 128), F32),
             pltpu.VMEM((3, 64, 128), F32),
-            pltpu.VMEM((3, 512, 128), F32),
-            pltpu.VMEM((7, 64, 128), F32),
-            pltpu.VMEM((2, 32, 128), F32),
+            pltpu.VMEM((2, 2, 2, 256, 128), F32),
+            pltpu.VMEM((7, 32, 128), F32),
+            pltpu.VMEM((32, 128), F32),
+            pltpu.VMEM((256, 128), F32),
             pltpu.VMEM((4, 8, 256), F32),
             pltpu.VMEM((8, 256), F32),
             pltpu.VMEM((8, 256), F32),
             pltpu.VMEM((NX, 8, 256), F32),
             pltpu.VMEM((NY, 8, 256), F32),
             dma((3,)), dma((3,)), dma((2,)), dma((2,)), dma((2, 2, 4)), dma((2, 2, 4)),
-            dma((3,)), dma((3,)), dma((3,)), dma((3,)), dma((7,)), dma((7,)), dma((2,)), dma((2,)),
+            dma((3,)), dma((3,)), dma((2, 2, 2)), dma((2, 2, 2)), dma((7,)), dma((7,)), dma((2,)), dma((2,)),
             dma((2,)), dma((2,)), dma((3,)), dma((3,)), dma((7,)), dma((7,)),
         ],
         compiler_params=pltpu.CompilerParams(
@@ -365,13 +404,22 @@
         cols,
         jnp.stack(shares),
     )
+    conv_grad, head_grad, occ_grad, cohort_grad, edu_grad, pred = pl.pallas_call(
+        place_kernel,
+        out_shape=(
+            jax.ShapeDtypeStruct((15, 2, 256), F32),
+            jax.ShapeDtypeStruct((3, 256), F32),
+            jax.ShapeDtypeStruct((840,), F32),
+            jax.ShapeDtypeStruct((40,), F32),
+            jax.ShapeDtypeStruct((8,), F32),
+            jax.ShapeDtypeStruct((2,), F32),
+        ),
+        in_specs=[vmem] * 3,
+        out_specs=(vmem,) * 5 + (smem,),
+        compiler_params=pltpu.CompilerParams(vmem_limit_bytes=2 * 1024 * 1024),
+    )(conv_grad, small, pred)
     return (
-        conv_grad[:, :15, :],
-        small[:3],
-        small[4:].reshape(1024)[:840],
-        small[3, :40],
-        small[3, 128:136],
-        pred[:2, 0],
+        jnp.transpose(conv_grad, (1, 0, 2)), head_grad, occ_grad, cohort_grad, edu_grad, pred
     )
 
 

time: 67.5 us -> 59 us (0.87)
  Pallas kernels: 54 us -> 48.9 us
  local copies, waits for them, and re-layouts: 6.8 us -> 3.32 us
    pallas_call x1, Pallas kernels: 54 us -> 48.3 us  [local(): pl.pallas_call(kernel, out_shape=(jax.ShapeDtypeStruct((2, 16, 256), F32)...]
    unnamed x35 -> x32, local copies, waits for them, and re-layouts: 3.32 us -> 2.08 us
    slice x2 -> x0, local copies, waits for them, and re-layouts: 1.22 us -> none  [the longest x1 0.63 us: local(): pred[:2, 0]]
    squeeze x2 -> x0, local copies, waits for them, and re-layouts: 1.03 us -> none  [the longest x1 0.51 us: local(): small[3, 128:136]]
where the time goes in v2:
time: 59 us; the launch traced here: 58.8 us
  Pallas kernels  48.9 us (83%)
  other arithmetic  3.49 us (6%)
  local copies, waits for them, and re-layouts  3.32 us (6%)
  matrix products  2.04 us (3%)
  between operations  1 us (2%)
    pallas_call x1, Pallas kernels, local(): pl.pallas_call(kernel, out_shape=(jax.ShapeDtypeStruct((2, 16, 256), F32)...  48.3 us
    unnamed x32, local copies, waits for them, and re-layouts  2.08 us
    dot_general x3, matrix products, convolve(): jnp.einsum('ptje,ejf->ptf', window, weights[:, first:first + taps, :], pr...  1.57 us

profile of v2, /device:TPU:1, one launch (start us, length us, event | category | flops | bytes accessed | tf_op | source)
XLA Modules:
  0.0 58.8 jit_solution(2950689849174678200)
XLA Ops:
  0.6 0.7 %iota_compare_fusion.3 = pred[2,256]{1,0:T(4,128)(4,1)S(1)} fusion(s32[2]{0:T(128)} %param.12), kind=kLoop, calls=%fused_computation.88 | loop fusion | flops 512 | bytes 520 | tf_op jit(solution)/shard_map/lt | solution.py:317
  1.4 1.2 %broadcast_select_fusion = bf16[2,256,256]{2,1,0:T(8,128)(2,1)S(1)} fusion(bf16[2,256,256]{2,1,0:T(8,128)(2,1)} %param.11, pred[2,256]{1,0:T(4,128)(4,1)S(1)} %iota_compare_fusion.3), kind=kLoop, calls=%fused_computation.52 | loop fusion | flops 131072 | bytes 524800 | tf_op jit(solution)/shard_map/jit(_where)/select_n | solution.py:318
  2.8 0.1 constant_dynamic-update-slice_fusion
  3.0 0.1 constant_dynamic-update-slice_fusion.4
  3.1 0.1 bitcast_dynamic-update-slice_fusion.10
  3.2 1.0 %copy-done.6 = bf16[256,15,256]{2,0,1:T(8,128)(2,1)S(1)} copy-done((bf16[256,15,256]{2,0,1:T(8,128)(2,1)S(1)}, bf16[256,15,256]{2,0,1:T(8,128)(2,1)}, u32[]{:S(2)}) %copy-start.6) | copy-done | bytes 1966104
  4.2 0.5 fusion.37
  4.7 0.1 fusion.19
  5.0 0.7 %fusion.36 = (f32[2,256]{1,0:T(2,128)S(1)}, f32[2,256,256]{2,1,0:T(8,128)S(1)}) fusion(bf16[2,256,7,256]{3,1,0,2:T(8,128)(2,1)S(1)} %bitcast_dynamic-update-slice_fusion.7, bf16[256,15,256]{2,0,1:T(8,128)(2,1)S(1)} %copy-done.6, pred[2,256]{1,0:T(4,128)(4,1)S(1)} %iota_compare_fusion.3), kind=kOutput, calls=%fused_computation.112 | convolution fusion | flops 470154752 | bytes 3279872 | tf_op jit(solution)/shard_map/ptje,ejf->ptf/dot_general | solution.py:22
  5.6 0.1 fusion.20
  5.7 0.2 divide_bitcast_fusion
  5.9 0.1 slice_bitcast_fusion.1
  6.0 0.1 fusion.42
  6.1 0.4 fusion.38
  6.7 0.1 pad_maximum_fusion.share_ref
  6.9 0.5 convolution_convert_fusion
  7.3 0.7 %pad_slice_fusion = (bf16[2,256,512]{2,1,0:T(8,128)(2,1)S(1)}, bf16[2,256,512]{2,1,0:T(8,128)(2,1)S(1)}, bf16[2,256,512]{2,1,0:T(8,128)(2,1)S(1)}, bf16[2,256,51...) fusion(bf16[2,256,512]{2,1,0:T(8,128)(2,1)S(1)} %convolution_convert_fusion), kind=kLoop, calls=%fused_computation.53 | loop fusion | bytes 3670016 | tf_op jit(solution)/shard_map/slice | solution.py:360
  8.5 0.4 copy-done
  8.9 0.1 pad_maximum_fusion.2
  9.1 0.2 fusion.25
  9.3 0.2 fusion.28
  9.5 0.2 fusion.29
  9.8 48.3 %shard_map.154 = (f32[2,16,256]{2,1,0:T(8,128)S(1)}, f32[8,256]{1,0:T(8,128)S(1)}, f32[8,128]{1,0:T(8,128)S(1)}) custom-call(s32[2]{0:T(128)S(1)} %copy-done.1, s32[2]{0:T(128)S(1)} %copy-done.2, s32[2]{0:T(128)S(1)} %copy-done.3, f32[3,8,128]{2,1,0:T(8,128)S(1)} %pad_maximum_fusion.1.rows_ref, f32[2,8,256]{2,1,0:T(8,128)S(1)} %pad.26.feat_ref, ...), custom_call_target="tpu_custom_call" | custom-call | tf_op jit(solution)/shard_map/pallas_call | solution.py:366
  58.1 0.6 %shard_map.155 = (f32[15,2,256]{2,1,0:T(2,128)}, f32[3,256]{1,0:T(4,128)}, f32[840]{0:T(1024)}, f32[40]{0:T(128)}, f32[8]{0:T(128)}, /*index=5*/f32[2]{0:T(128)}) custom-call(f32[2,16,256]{2,1,0:T(8,128)S(1)} %get-tuple-element.15.conv_ref, f32[8,256]{1,0:T(8,128)S(1)} %get-tuple-element.16.small_ref, f32[8,128]{1,0:T(8,128)S(1)} %get-tuple-element.17.pred_ref), custom_call_target="tpu_custom_call" | custom-call | tf_op jit(solution)/shard_map/pallas_call | solution.py:407
  (50 shorter events, 1.2 us)
Async XLA Ops:
  1.4 1.6 %copy-start.4 = (bf16[2,256,256]{2,1,0:T(8,128)(2,1)S(1)}, bf16[2,256,256]{2,1,0:T(8,128)(2,1)}, u32[]{:S(2)}) copy-start(bf16[2,256,256]{2,1,0:T(8,128)(2,1)} %param.11) | copy-start | bytes 786436
  2.7 1.5 %copy-start.6 = (bf16[256,15,256]{2,0,1:T(8,128)(2,1)S(1)}, bf16[256,15,256]{2,0,1:T(8,128)(2,1)}, u32[]{:S(2)}) copy-start(bf16[256,15,256]{2,0,1:T(8,128)(2,1)} %param.13) | copy-start | bytes 5898244
  8.2 0.7 %copy-start = (bf16[3,256]{1,0:T(4,128)(2,1)S(1)}, bf16[3,256]{1,0:T(4,128)(2,1)}, u32[]{:S(2)}) copy-start(bf16[3,256]{1,0:T(4,128)(2,1)} %head_ref.1) | copy-start | bytes 4612
  8.2 0.9 %copy-start.1 = (s32[2]{0:T(128)S(1)}, s32[2]{0:T(128)}, u32[]{:S(2)}) copy-start(s32[2]{0:T(128)} %occ_ref.1) | copy-start | bytes 28
  8.2 0.9 %copy-start.5 = (f32[840]{0:T(1024)S(1)}, f32[840]{0:T(1024)}, u32[]{:S(2)}) copy-start(f32[840]{0:T(1024)} %param.18) | copy-start | bytes 10084
  8.2 1.0 %copy-start.2 = (s32[2]{0:T(128)S(1)}, s32[2]{0:T(128)}, u32[]{:S(2)}) copy-start(s32[2]{0:T(128)} %coh_ref.1) | copy-start | bytes 28
  8.2 1.0 %copy-start.7 = (f32[40]{0:T(128)S(1)}, f32[40]{0:T(128)}, u32[]{:S(2)}) copy-start(f32[40]{0:T(128)} %param.19) | copy-start | bytes 484
  8.3 1.2 %copy-start.3 = (s32[2]{0:T(128)S(1)}, s32[2]{0:T(128)}, u32[]{:S(2)}) copy-start(s32[2]{0:T(128)} %edu_ref.1) | copy-start | bytes 28
  8.3 1.2 %copy-start.8 = (f32[8]{0:T(128)S(1)}, f32[8]{0:T(128)}, u32[]{:S(2)}) copy-start(f32[8]{0:T(128)} %param.20) | copy-start | bytes 100
  8.3 1.5 %copy-start.9 = (f32[2]{0:T(128)S(1)}, f32[2]{0:T(128)}, u32[]{:S(2)}) copy-start(f32[2]{0:T(128)} %param.21) | copy-start | bytes 28
